TPU v7x, 32 devices: a whole 2x2x4 slice. The times are simulated.
32 devices in a mesh: groups: 2 (over y), seq: 4 (over z), fsdp: 2 (over x), head: 2 (over core).
Axes of the slice: x: 2, y: 2, z: 4, core: 2. Of those that a mesh axis runs over, the one named last changes fastest.
Arguments:
- frames: bfloat16 [6144, 3072], P(('groups', 'seq')), parts along dimension 0, may hold values from -330 to 330
- modulation: float32 [4, 3072], P('groups'), parts along dimension 0, may hold values from -2.5 to 2.5
- w_qkv: bfloat16 [3072, 3, 2048], P('seq', None, ('fsdp', 'head')), may hold values from -0.109375 to 0.109375
- b_qkv: float32 [3, 2048], P(None, ('fsdp', 'head')), may hold values from -2.5 to 2.5
- qk_gain: float32 [2, 128], replicated, may hold values from 0.7 to 2.4
- block_lists: int32 [16, 27], P(('groups', 'seq')), parts along dimension 0, may hold values from -1 to 7, as said below
Outputs:
- attention: bfloat16 [6144, 2048], P(('groups', 'seq'), ('fsdp', 'head')), parts along dimension 0
There are 2 independent parts, one for each index of `groups`. A program takes and returns all parts, laid end to end along the dimension named above; an argument that names none is the same for every part. Nothing has to cross between parts.
Inputs may be any that keep to these rules, and one draw needn't show every extreme that they name: `block_lists`: tile g lies at width g // 2, time (g % 2) // 1 and height g % 1 of a 2 x 1 x 4 grid of tiles. Entry (a + 1) * 9 + (b + 1) * 3 + (c + 1) of row g, for a, b, c in -1, 0, 1, is the tile at time + a, height + b and width + c of tile g, or -1 where that tile is outside the grid or left out of the list. Entry 13 is always g.
All inputs are finite; a program needn't handle non-finite values.
Results may differ from a plain program's by a relative error of at most 0.0058.
Values may be sent and summed in bfloat16 or wider, within the bound.
No kernel may reach another device: no remote copies, remote signals or barrier semaphores. Data moves between devices by JAX's collectives and lax.ppermute only.
A program may use at most 128 MiB of HBM per device.

v0:
```python
import math
import jax
import jax.numpy as jnp
from jax import lax
from jax.sharding import PartitionSpec as P


def with_halo(shard, sides, width):
    for axis, dim in sides:
        devices, length = (lax.axis_size(axis), shard.shape[dim])
        up = [(i, (i + 1) % devices) for i in range(devices - 1)]
        down = [(j, i) for i, j in up]
        last = lax.slice_in_dim(shard, length - width, length, axis=dim)
        first = lax.slice_in_dim(shard, 0, width, axis=dim)
        before = lax.ppermute(last, axis, up)
        after = lax.ppermute(first, axis, down)
        shard = jnp.concatenate([before, shard, after], axis=dim)
    return shard


def normed_heads(tensor, gain_row, head_dim):
    shaped = tensor.reshape(tensor.shape[0], tensor.shape[1] // head_dim, head_dim)
    scaled = (
        shaped * lax.rsqrt(jnp.mean(shaped * shaped, axis=-1, keepdims=True) + 1e-06) * gain_row
    )
    return scaled.astype(jnp.bfloat16)


def reach_sides(key_rows, values):
    stacked = jnp.stack([key_rows, values], axis=0)
    return with_halo(stacked, (("seq", 1),), key_rows.shape[0])


def per_device(frames, modulation, w_qkv, b_qkv, qk_gain, block_lists):
    inputs = frames.astype(jnp.float32)
    average = jnp.mean(inputs, axis=-1, keepdims=True)
    centred = inputs - average
    variance = jnp.mean(centred * centred, axis=-1, keepdims=True)
    normed = centred * lax.rsqrt(variance + 1e-06) * (1.0 + modulation[0]) + modulation[1]
    normed = normed.astype(jnp.bfloat16)
    tokens = normed.shape[0]
    width_cols = w_qkv.shape[2]
    head_dim = qk_gain.shape[1]
    heads = width_cols // head_dim
    projected = jnp.einsum(
        "td,djc->tjc",
        normed,
        lax.all_gather(w_qkv, "seq", axis=0, tiled=True),
        preferred_element_type=jnp.float32,
    )
    projected = projected + b_qkv
    queries = normed_heads(projected[:, 0], qk_gain[0], head_dim)
    key_rows = normed_heads(projected[:, 1], qk_gain[1], head_dim)
    values = projected[:, 2].astype(jnp.bfloat16).reshape(tokens, heads, head_dim)
    neighbourhood = reach_sides(key_rows, values)
    position = lax.axis_index("seq")
    tile_dev = block_lists.shape[0]
    tile_len = tokens // tile_dev
    candidates = (position - 1) * tile_dev + jnp.arange(3 * tile_dev, dtype=jnp.int32)
    matches = (block_lists[:, :, None] == candidates[None, None, :]) & (
        block_lists[:, :, None] >= 0
    )
    allowed_tiles = jnp.any(matches, axis=1)
    allowed_keys = jnp.repeat(jnp.repeat(allowed_tiles, tile_len, axis=0), tile_len, axis=1)
    factor = 1.0 / math.sqrt(head_dim)
    scores = (
        jnp.einsum("qhd,khd->hqk", queries, neighbourhood[0], preferred_element_type=jnp.float32)
        * factor
    )
    weights = jnp.where(allowed_keys[None, :, :], jnp.exp(scores), 0.0)
    totals = jnp.sum(weights, axis=-1)
    mixture = jnp.einsum(
        "hqk,khd->qhd",
        weights.astype(jnp.bfloat16),
        neighbourhood[1],
        preferred_element_type=jnp.float32,
    )
    result = (mixture / jnp.transpose(totals)[:, :, None]).astype(jnp.bfloat16)
    return result.reshape(tokens, width_cols)


def solution(mesh):
    placed = (
        P(("groups", "seq"), None),
        P("groups", None),
        P("seq", None, ("fsdp", "head")),
        P(None, ("fsdp", "head")),
        P(),
        P(("groups", "seq"), None),
    )
    return jax.shard_map(
        per_device,
        mesh=mesh,
        in_specs=placed,
        out_specs=P(("groups", "seq"), ("fsdp", "head")),
        check_vma=False,
    )
```

profile of v0, /device:TPU:0, one launch (start us, length us, event | category | flops | bytes accessed | tf_op | source)
XLA Modules:
  0.0 278.2 jit_solution(9089081699902757114)
XLA Ops:
  6.5 0.0 copy-start.6
  6.5 0.0 all-gather.2.cloned.1.call-start
  6.5 4.3 %copy.27 = bf16[768,3,512]{0,2,1:T(8,128)(2,1)} copy(bf16[768,3,512]{2,0,1:T(8,128)(2,1)} %param.8) | data formatting | bytes 4718592 | tf_op args[2]
  10.8 0.0 all-gather.2.cloned.1.call-update
  10.9 0.0 copy-done.6
  10.9 0.0 copy-start
  10.9 0.0 copy-start.5
  10.9 0.0 copy-start.8
  10.9 3.2 %convert_reduce_fusion = f32[768]{0:T(1024)S(1)} fusion(bf16[768,3072]{1,0:T(8,128)(2,1)} %param.6), kind=kLoop, calls=%fused_computation.6 | loop fusion | flops 4717824 | bytes 4721664 | tf_op jit(solution)/shard_map/reduce_sum | solution.py:36
  14.1 0.5 copy-done
  14.6 1.4 fusion.7
  16.0 0.0 copy-done.5
  16.0 164.5 %all-gather.2.cloned.1.call-done = bf16[3072,3,512]{0,2,1:T(8,128)(2,1)} async-done(((bf16[768,3,512]{0,2,1:T(8,128)(2,1)}), bf16[3072,3,512]{0,2,1:T(8,128)(2,1)}) %all-gather.2.cloned.1.call-update) | async-done | bytes 9437200 | tf_op jit(solution)/shard_map/all_gather | solution.py:48
  180.5 0.0 copy-done.8
  180.5 11.9 %broadcast_add_fusion = f32[768,3,512]{0,2,1:T(8,128)S(1)} fusion(f32[3,512]{1,0:T(4,128)S(1)} %copy-done.8, bf16[3072,3,512]{0,2,1:T(8,128)(2,1)} %all-gather.2.cloned.1.call-done, bf16[768,3072]{1,0:T(8,128)(2,1)} %param.6, f32[3072]{0:T(1024)S(1)} %bitcast.43, f32[3072]{0:T(1024)S(1)} %bitcast.42, f32[768]{0:T(1024)S(1)} %add_rsqrt_fusion.2, ...), kind=kOutput, calls=%fused_computation.23 | convolution fusion | flops 7263092736 | bytes 18911232 | tf_op jit(solution)/shard_map/td,djc->tjc/dot_general | solution.py:45
  192.4 0.1 slice.53
  192.5 2.0 fusion.28
  194.5 0.4 copy.29
  194.9 1.5 reduce_sum.47
  196.4 0.0 copy-start.7
  196.4 3.0 %copy.28 = f32[1,768,4,128]{3,1,2,0:T(8,128)} copy(f32[1,768,4,128]{1,3,2,0:T(8,128)} %bitcast.37) | data formatting | bytes 3145728 | tf_op jit(solution)/shard_map/reshape;squeeze | solution.py:22
  199.5 1.9 multiply_convert_fusion.1
  201.4 1.3 pad_maximum_fusion.1
  202.6 1.3 collective-permute-start.1
  203.9 5.7 %collective-permute-start = (bf16[2,768,4,128]{3,1,2,0:T(8,128)(2,1)}, bf16[2,768,4,128]{3,1,2,0:T(8,128)(2,1)}, u32[]{:S(2)}, u32[]{:S(2)}) collective-permute-start(bf16[2,768,4,128]{3,1,2,0:T(8,128)(2,1)} %pad_maximum_fusion.1), channel_id=1, source_target_pairs={{0,4},{4,8},{8,12},{1,5},{5,9},{9,13},{2,6},{6,10},{10,14},{3,7},{... | collective-permute-start | bytes 4718600 | tf_op jit(solution)/shard_map/ppermute | solution.py:15
  209.7 0.0 copy-done.7
  209.7 0.2 and_reduce_fusion
  209.9 0.1 broadcast_in_dim.14
  209.9 1.7 broadcast_in_dim.19
  211.6 5.4 %copy.30 = pred[768,2304]{1,0:T(8,128)(4,1)} copy(pred[768,2304]{0,1:T(8,128)(4,1)} %bitcast.36) | data formatting | bytes 3538944 | tf_op jit(solution)/shard_map/jit(_where)/broadcast_in_dim | solution.py:70
  217.0 1.6 copy.31
  218.6 0.1 multiply_reduce_fusion
  218.8 0.0 copy-start.2
  218.8 0.0 copy-start.4
  218.8 22.4 %collective-permute-done.1 = bf16[2,768,4,128]{3,1,2,0:T(8,128)(2,1)} collective-permute-done((bf16[2,768,4,128]{3,1,2,0:T(8,128)(2,1)}, bf16[2,768,4,128]{3,1,2,0:T(8,128)(2,1)}, u32[]{:S(2)}, u32[]{:S(2)}) %collective-permute-start.1) | collective-permute-done | bytes 1572896 | tf_op jit(solution)/shard_map/ppermute | solution.py:16
  241.2 1.2 collective-permute-done
  242.4 2.0 pad_maximum_fusion
  244.4 0.0 copy-start.1
  244.4 0.0 copy-done.2
  244.4 0.0 copy-done.4
  244.4 0.0 copy-start.3
  244.4 12.9 %fusion = (f32[4,768]{1,0:T(4,128)S(1)}, f32[4,768,2304]{2,1,0:T(8,128)}) fusion(pred[768,2304]{1,0:T(8,128)(4,1)S(1)} %copy-done.2, bf16[2,2304,4,128]{3,1,2,0:T(8,128)(2,1)S(1)} %pad_maximum_fusion, f32[768,4,128]{2,0,1:T(8,128)S(1)} %copy-done.4, f32[128]{0:T(128)S(1)} %get-tuple-element.10, f32[768,4]{0,1:T(4,128)S(1)} %add_rsqrt_fusion), kind=kOutput, calls=%fused_computation.1 | convolution fusion | flops 1834349568 | bytes 34038272 | tf_op jit(solution)/shard_map/qhd,khd->hqk/dot_general | solution.py:67
  257.3 0.0 copy-done.1
  257.3 0.0 copy-done.3
  257.3 12.9 %fusion.21 = bf16[768,4,128]{0,2,1:T(8,128)(2,1)S(1)} fusion(f32[768,4]{0,1:T(4,128)S(1)} %bitcast.44, f32[4,768,2304]{2,1,0:T(8,128)} %get-tuple-element.13, pred[768,2304]{1,0:T(8,128)(4,1)S(1)} %copy-done.3, bf16[2,2304,4,128]{3,1,2,0:T(8,128)(2,1)} %copy-done.1), kind=kOutput, calls=%fused_computation.27 | convolution fusion | flops 1833959424 | bytes 33239040 | tf_op jit(solution)/shard_map/hqk,khd->qhd/dot_general | solution.py:72
  270.2 1.2 copy.33
  (8 shorter events, 0.1 us)
Async XLA Ops:
  6.5 4.3 %copy-start.6 = (f32[2,128]{1,0:T(2,128)S(1)}, f32[2,128]{1,0:T(2,128)}, u32[]{:S(2)}) copy-start(f32[2,128]{1,0:T(2,128)} %param.10) | copy-start | bytes 3076
  6.5 174.0 %all-gather.2.cloned.1.call-start = ((), (), s32[]{:S(2)}) async-start(), calls=%async_computation | async-start | bytes 11796480 | tf_op jit(solution)/shard_map/all_gather | solution.py:48
  10.9 3.8 %copy-start = (bf16[768,3072]{1,0:T(8,128)(2,1)S(1)}, bf16[768,3072]{1,0:T(8,128)(2,1)}, u32[]{:S(2)}) copy-start(bf16[768,3072]{1,0:T(8,128)(2,1)} %param.6) | copy-start | bytes 14155780
  10.9 5.1 %copy-start.5 = (f32[2,3072]{1,0:T(2,128)S(1)}, f32[2,3072]{1,0:T(2,128)}, u32[]{:S(2)}) copy-start(f32[2,3072]{1,0:T(2,128)} %param.7) | copy-start | bytes 73732
  10.9 169.6 %copy-start.8 = (f32[3,512]{1,0:T(4,128)S(1)}, f32[3,512]{1,0:T(4,128)}, u32[]{:S(2)}) copy-start(f32[3,512]{1,0:T(4,128)} %param.9) | copy-start | bytes 18436
  196.4 13.3 %copy-start.7 = (s32[2,27]{1,0:T(2,128)S(1)}, s32[2,27]{1,0:T(2,128)}, u32[]{:S(2)}) copy-start(s32[2,27]{1,0:T(2,128)} %param.11) | copy-start | bytes 652
  202.6 38.6 %collective-permute-start.1 = (bf16[2,768,4,128]{3,1,2,0:T(8,128)(2,1)}, bf16[2,768,4,128]{3,1,2,0:T(8,128)(2,1)}, u32[]{:S(2)}, u32[]{:S(2)}) collective-permute-start(bf16[2,768,4,128]{3,1,2,0:T(8,128)(2,1)} %pad_maximum_fusion.1), channel_id=1, source_target_pairs={{4,0},{8,4},{12,8},{5,1},{9,5},{13,9},{6,2},{10,6},{14,10},{7,3},{... | collective-permute-start | bytes 4718600 | tf_op jit(solution)/shard_map/ppermute | solution.py:16
  203.9 38.4 %collective-permute-start = (bf16[2,768,4,128]{3,1,2,0:T(8,128)(2,1)}, bf16[2,768,4,128]{3,1,2,0:T(8,128)(2,1)}, u32[]{:S(2)}, u32[]{:S(2)}) collective-permute-start(bf16[2,768,4,128]{3,1,2,0:T(8,128)(2,1)} %pad_maximum_fusion.1), channel_id=1, source_target_pairs={{0,4},{4,8},{8,12},{1,5},{5,9},{9,13},{2,6},{6,10},{10,14},{3,7},{... | collective-permute-start | bytes 4718600 | tf_op jit(solution)/shard_map/ppermute | solution.py:15
  218.8 25.6 %copy-start.2 = (pred[768,2304]{1,0:T(8,128)(4,1)S(1)}, pred[768,2304]{1,0:T(8,128)(4,1)}, u32[]{:S(2)}) copy-start(pred[768,2304]{1,0:T(8,128)(4,1)} %copy.30) | copy-start | bytes 5308420
  218.8 25.6 %copy-start.4 = (f32[768,4,128]{2,0,1:T(8,128)S(1)}, f32[768,4,128]{2,0,1:T(8,128)}, u32[]{:S(2)}) copy-start(f32[768,4,128]{2,0,1:T(8,128)} %copy.31) | copy-start | bytes 4718596
  244.4 12.9 %copy-start.1 = (bf16[2,2304,4,128]{3,1,2,0:T(8,128)(2,1)}, bf16[2,2304,4,128]{3,1,2,0:T(8,128)(2,1)S(1)}, u32[]{:S(2)}) copy-start(bf16[2,2304,4,128]{3,1,2,0:T(8,128)(2,1)S(1)} %pad_maximum_fusion) | copy-start | bytes 14155780
  244.4 12.9 %copy-start.3 = (pred[768,2304]{1,0:T(8,128)(4,1)S(1)}, pred[768,2304]{1,0:T(8,128)(4,1)}, u32[]{:S(2)}) copy-start(pred[768,2304]{1,0:T(8,128)(4,1)} %copy.30) | copy-start | bytes 5308420
Sparse Core Ops, SparseCore 0:
  11.0 169.4 all-gather.1
where the time goes:
time: 279 us; the launch traced here: 278 us
  waiting for transfers between devices  188 us (67%)
  matrix products  37.7 us (14%)
  local copies, waits for them, and re-layouts  18.3 us (7%)
  other arithmetic  13.7 us (5%)
  between operations  13.6 us (5%)
  starting transfers between devices  7 us (3%)
    all_gather x1, waiting for transfers between devices, per_device(): lax.all_gather(w_qkv, 'seq', axis=0, tiled=True)  164 us
    ppermute x1, waiting for transfers between devices, with_halo(): after = lax.ppermute(first, axis, down)  22.4 us
    dot_general x1, matrix products, per_device(): jnp.einsum('qhd,khd->hqk', queries, neighbourhood[0], preferred_element_t...  12.9 us
    dot_general x1, matrix products, per_device(): jnp.einsum('hqk,khd->qhd', weights.astype(jnp.bfloat16), neighbourhood[1]...  12.9 us
    dot_general x1, matrix products, per_device(): jnp.einsum('td,djc->tjc', normed, lax.all_gather(w_qkv, 'seq', axis=0, ti...  11.9 us
    ppermute x1, starting transfers between devices, with_halo(): before = lax.ppermute(last, axis, up)  5.72 us
  transfers between devices with their start and end apart: 3, of which 3 were waited for; matrix products, arithmetic and copies ran while one was open for 5% of the time, Pallas kernels for 0%

commit v1 on v0

--- a/solution.py
+++ b/solution.py
@@ -3,6 +3,22 @@
 import jax.numpy as jnp
 from jax import lax
 from jax.sharding import PartitionSpec as P
+
+
+def product_in_turn(x, axis, dim, contribution):
+    size, index, extent = (lax.axis_size(axis), lax.axis_index(axis), x.shape[dim])
+    right = [(i, (i + 1) % size) for i in range(size)]
+    behind = [(i, (i - 1) % size) for i in range(size)]
+    halfway = size // 2
+    from_left = from_right = x
+    running = contribution(x, index * extent)
+    for hop in range(1, halfway + 1):
+        from_left = lax.ppermute(from_left, axis, right)
+        if hop < size - halfway:
+            from_right = lax.ppermute(from_right, axis, behind)
+            running = running + contribution(from_right, (index + hop) % size * extent)
+        running = running + contribution(from_left, (index - hop) % size * extent)
+    return running
 
 
 def with_halo(shard, sides, width):
@@ -42,11 +58,16 @@
     width_cols = w_qkv.shape[2]
     head_dim = qk_gain.shape[1]
     heads = width_cols // head_dim
-    projected = jnp.einsum(
-        "td,djc->tjc",
-        normed,
-        lax.all_gather(w_qkv, "seq", axis=0, tiled=True),
-        preferred_element_type=jnp.float32,
+    projected = product_in_turn(
+        w_qkv,
+        "seq",
+        0,
+        lambda part, start: jnp.einsum(
+            "td,djc->tjc",
+            lax.dynamic_slice_in_dim(normed, start, part.shape[0], axis=1),
+            part,
+            preferred_element_type=jnp.float32,
+        ),
     )
     projected = projected + b_qkv
     queries = normed_heads(projected[:, 0], qk_gain[0], head_dim)

time: 279 us -> 242 us (0.87)
  waiting for transfers between devices: 188 us -> 154 us
  between operations: 13.6 us -> 0.32 us
  starting transfers between devices: 7 us -> 12.2 us
  other arithmetic: 13.7 us -> 18.8 us
    all_gather x1 -> x0, waiting for transfers between devices: 164 us -> none  [per_device(): lax.all_gather(w_qkv, 'seq', axis=0, tiled=True)]
    ppermute x0 -> x3, waiting for transfers between devices: none -> 133 us  [the longest x2 94.9 us: product_in_turn(): from_left = lax.ppermute(from_left, axis, right)]
    ppermute x0 -> x3, starting transfers between devices: none -> 5.17 us  [the longest x2 3.08 us: product_in_turn(): from_left = lax.ppermute(from_left, axis, right)]
    convert_element_type x0 -> x1, other arithmetic: none -> 5.13 us  [per_device(): normed = normed.astype(jnp.bfloat16)]
    dot_general x1 -> x4, matrix products: 11.9 us -> 13.4 us  [per_device(): jnp.einsum('td,djc->tjc', lax.dynamic_slice_in_dim(normed, start, part.sh...]
  transfers between devices with their start and end apart: 3 -> 5, of which waited for: 3 -> 5; matrix products, arithmetic and copies ran while one was open for 5% -> 12% of each run, Pallas kernels for 0% -> 0%
where the time goes in v1:
time: 242 us; the launch traced here: 241 us
  waiting for transfers between devices  154 us (64%)
  matrix products  39.2 us (16%)
  other arithmetic  18.8 us (8%)
  local copies, waits for them, and re-layouts  16.3 us (7%)
  starting transfers between devices  12.2 us (5%)
    ppermute x2, waiting for transfers between devices, product_in_turn(): from_left = lax.ppermute(from_left, axis, right)  94.9 us
    ppermute x1, waiting for transfers between devices, product_in_turn(): from_right = lax.ppermute(from_right, axis, behind)  38.3 us
    ppermute x1, waiting for transfers between devices, with_halo(): after = lax.ppermute(first, axis, down)  19.8 us
    dot_general x4, matrix products, per_device(): jnp.einsum('td,djc->tjc', lax.dynamic_slice_in_dim(normed, start, part.sh...  13.4 us
    dot_general x1, matrix products, per_device(): jnp.einsum('hqk,khd->qhd', weights.astype(jnp.bfloat16), neighbourhood[1]...  12.9 us
    dot_general x1, matrix products, per_device(): jnp.einsum('qhd,khd->hqk', queries, neighbourhood[0], preferred_element_t...  12.8 us
    ppermute x1, starting transfers between devices, with_halo(): before = lax.ppermute(last, axis, up)  5.73 us
    broadcast_in_dim x1, local copies, waits for them, and re-layouts, per_device(): weights = jnp.where(allowed_keys[None, :, :], jnp.exp(scores), 0.0)  5.39 us
  transfers between devices with their start and end apart: 5, of which 5 were waited for; matrix products, arithmetic and copies ran while one was open for 12% of the time, Pallas kernels for 0%

profile of v1, /device:TPU:0, one launch (start us, length us, event | category | flops | bytes accessed | tf_op | source)
XLA Modules:
  0.0 241.0 jit_solution(15746195288642044438)
XLA Ops:
  0.0 2.8 %copy.34 = bf16[768,3,512]{0,2,1:T(8,128)(2,1)S(1)} copy(bf16[768,3,512]{2,0,1:T(8,128)(2,1)} %param.8) | data formatting | bytes 4718592 | tf_op args[2]
  2.9 0.0 copy-start
  2.9 0.0 copy-start.8
  2.9 3.1 %collective-permute-start.1 = (bf16[768,3,512]{0,2,1:T(8,128)(2,1)S(1)}, bf16[768,3,512]{0,2,1:T(8,128)(2,1)}, u32[]{:S(2)}, u32[]{:S(2)}) collective-permute-start(bf16[768,3,512]{0,2,1:T(8,128)(2,1)S(1)} %copy.34), channel_id=1, source_target_pairs={{0,4},{4,8},{8,12},{12,0},{1,5},{5,9},{9,13},{13,1},{2,6},{6,10},{... | collective-permute-start | bytes 7077896 | tf_op jit(solution)/shard_map/ppermute | solution.py:16
  6.0 2.1 collective-permute-start
  8.0 3.0 %convert_reduce_fusion = f32[768]{0:T(1024)S(1)} fusion(bf16[768,3072]{1,0:T(8,128)(2,1)} %param.6), kind=kLoop, calls=%fused_computation.6 | loop fusion | flops 4717824 | bytes 4721664 | tf_op jit(solution)/shard_map/reduce_sum | solution.py:52
  11.1 0.0 copy-done.7
  11.1 0.0 copy-done
  11.1 1.4 fusion.7
  12.5 47.7 %collective-permute-done.1 = bf16[768,3,512]{0,2,1:T(8,128)(2,1)} collective-permute-done((bf16[768,3,512]{0,2,1:T(8,128)(2,1)S(1)}, bf16[768,3,512]{0,2,1:T(8,128)(2,1)}, u32[]{:S(2)}, u32[]{:S(2)}) %collective-permute-start.1) | collective-permute-done | bytes 2359328 | tf_op jit(solution)/shard_map/ppermute | solution.py:16
  60.2 0.0 collective-permute-start.2
  60.2 0.0 copy-done.8
  60.3 0.0 copy-start.2
  60.3 5.1 %fusion.10 = bf16[768,3072]{1,0:T(8,128)(2,1)S(1)} fusion(bf16[768,3072]{1,0:T(8,128)(2,1)} %param.6, f32[3072]{0:T(1024)S(1)} %bitcast.52, f32[3072]{0:T(1024)S(1)} %bitcast.51, f32[768]{0:T(1024)S(1)} %add_rsqrt_fusion.2, f32[768]{0:T(1024)S(1)} %broadcast_multiply_fusion), kind=kLoop, calls=%fused_computation.12 | loop fusion | flops 14155776 | bytes 9467904 | tf_op jit(solution)/shard_map/convert_element_type | solution.py:56
  65.4 0.0 copy-done.2
  65.4 2.0 fusion.18
  67.5 3.7 %fusion.14 = f32[768,3,512]{0,2,1:T(8,128)S(1)} fusion(bf16[768,3,512]{0,2,1:T(8,128)(2,1)} %collective-permute-done.1, bf16[768,3072]{1,0:T(8,128)(2,1)S(1)} %fusion.10, s32[]{:T(128)S(6)} %select_n.35), kind=kOutput, calls=%fused_computation.26 | convolution fusion | flops 1811939328 | bytes 8257540 | tf_op jit(solution)/shard_map/td,djc->tjc/dot_general | solution.py:65
  71.2 0.0 copy-start.6
  71.2 38.3 %collective-permute-done = bf16[768,3,512]{0,2,1:T(8,128)(2,1)} collective-permute-done((bf16[768,3,512]{0,2,1:T(8,128)(2,1)S(1)}, bf16[768,3,512]{0,2,1:T(8,128)(2,1)}, u32[]{:S(2)}, u32[]{:S(2)}) %collective-permute-start) | collective-permute-done | bytes 2359328 | tf_op jit(solution)/shard_map/ppermute | solution.py:18
  109.5 3.7 %fusion.16 = f32[768,3,512]{0,2,1:T(8,128)S(1)} fusion(bf16[768,3,512]{0,2,1:T(8,128)(2,1)} %collective-permute-done, bf16[768,3072]{1,0:T(8,128)(2,1)S(1)} %fusion.10, s32[]{:T(128)S(6)} %select_n.33), kind=kOutput, calls=%fused_computation.28 | convolution fusion | flops 1811939328 | bytes 8257540 | tf_op jit(solution)/shard_map/td,djc->tjc/dot_general | solution.py:65
  113.3 47.2 %collective-permute-done.2 = bf16[768,3,512]{0,2,1:T(8,128)(2,1)} collective-permute-done((bf16[768,3,512]{0,2,1:T(8,128)(2,1)}, bf16[768,3,512]{0,2,1:T(8,128)(2,1)}, u32[]{:S(2)}, u32[]{:S(2)}) %collective-permute-start.2) | collective-permute-done | bytes 2359328 | tf_op jit(solution)/shard_map/ppermute | solution.py:16
  160.5 4.0 %add_add_fusion = f32[768,3,512]{0,2,1:T(8,128)S(1)} fusion(f32[768,3,512]{0,2,1:T(8,128)S(1)} %fusion.14, f32[768,3,512]{0,2,1:T(8,128)S(1)} %fusion.18, f32[768,3,512]{0,2,1:T(8,128)S(1)} %fusion.16, f32[3,512]{1,0:T(4,128)S(1)} %copy-done.6, bf16[768,3,512]{0,2,1:T(8,128)(2,1)} %collective-permute-done.2, bf16[768,3072]{1,0:T(8,128)(2,1)S(1)} %fusion.10, ...), kind=kOutput, calls=%fused_computation.14 | convolution fusion | flops 1816657920 | bytes 22421508 | tf_op jit(solution)/shard_map/td,djc->tjc/dot_general | solution.py:65
  164.5 0.1 slice.53
  164.6 2.0 fusion.34
  166.6 0.4 copy.37
  167.0 1.5 reduce_sum.47
  168.5 0.0 copy-start.9
  168.5 3.0 %copy.36 = f32[1,768,4,128]{3,1,2,0:T(8,128)} copy(f32[1,768,4,128]{1,3,2,0:T(8,128)} %bitcast.47) | data formatting | bytes 3145728 | tf_op jit(solution)/shard_map/reshape;squeeze | solution.py:38
  171.5 1.9 multiply_convert_fusion.1
  173.4 1.5 pad_maximum_fusion.1
  174.9 1.3 collective-permute-start.4
  176.2 5.7 %collective-permute-start.3 = (bf16[2,768,4,128]{3,1,2,0:T(8,128)(2,1)}, bf16[2,768,4,128]{3,1,2,0:T(8,128)(2,1)}, u32[]{:S(2)}, u32[]{:S(2)}) collective-permute-start(bf16[2,768,4,128]{3,1,2,0:T(8,128)(2,1)} %pad_maximum_fusion.1), channel_id=1, source_target_pairs={{0,4},{4,8},{8,12},{1,5},{5,9},{9,13},{2,6},{6,10},{10,14},{3,7},{... | collective-permute-start | bytes 4718600 | tf_op jit(solution)/shard_map/ppermute | solution.py:31
  182.0 0.2 and_reduce_fusion
  182.1 0.1 broadcast_in_dim.14
  182.2 1.7 broadcast_in_dim.19
  183.9 5.4 %copy.38 = pred[768,2304]{1,0:T(8,128)(4,1)} copy(pred[768,2304]{0,1:T(8,128)(4,1)} %bitcast.46) | data formatting | bytes 3538944 | tf_op jit(solution)/shard_map/jit(_where)/broadcast_in_dim | solution.py:91
  189.3 1.6 copy.39
  190.9 0.1 multiply_reduce_fusion
  191.1 19.8 %collective-permute-done.4 = bf16[2,768,4,128]{3,1,2,0:T(8,128)(2,1)} collective-permute-done((bf16[2,768,4,128]{3,1,2,0:T(8,128)(2,1)}, bf16[2,768,4,128]{3,1,2,0:T(8,128)(2,1)}, u32[]{:S(2)}, u32[]{:S(2)}) %collective-permute-start.4) | collective-permute-done | bytes 1572896 | tf_op jit(solution)/shard_map/ppermute | solution.py:32
  210.9 1.2 collective-permute-done.3
  212.1 2.0 pad_maximum_fusion
  214.1 0.0 copy-start.1
  214.1 0.0 copy-done.3
  214.1 0.0 copy-done.5
  214.1 0.0 copy-start.4
  214.1 12.8 %fusion = (f32[4,768]{1,0:T(4,128)S(1)}, f32[4,768,2304]{2,1,0:T(8,128)}) fusion(pred[768,2304]{1,0:T(8,128)(4,1)S(1)} %copy-done.3, bf16[2,2304,4,128]{3,1,2,0:T(8,128)(2,1)S(1)} %pad_maximum_fusion, f32[768,4,128]{2,0,1:T(8,128)S(1)} %copy-done.5, f32[128]{0:T(128)S(1)} %get-tuple-element.10, f32[768,4]{0,1:T(4,128)S(1)} %add_rsqrt_fusion), kind=kOutput, calls=%fused_computation.1 | convolution fusion | flops 1834349568 | bytes 34038272 | tf_op jit(solution)/shard_map/qhd,khd->hqk/dot_general | solution.py:88
  227.0 12.9 %fusion.12 = bf16[768,4,128]{0,2,1:T(8,128)(2,1)S(1)} fusion(f32[768,4]{0,1:T(4,128)S(1)} %bitcast.54, f32[4,768,2304]{2,1,0:T(8,128)} %get-tuple-element.13, pred[768,2304]{1,0:T(8,128)(4,1)S(1)} %copy-done.4, bf16[2,2304,4,128]{3,1,2,0:T(8,128)(2,1)} %copy-done.1), kind=kOutput, calls=%fused_computation.21 | convolution fusion | flops 1833959424 | bytes 33239040 | tf_op jit(solution)/shard_map/hqk,khd->qhd/dot_general | solution.py:93
  239.9 1.2 copy.41
  (15 shorter events, 0.1 us)
Async XLA Ops:
  0.0 11.1 %copy-start.7 = (f32[2,3072]{1,0:T(2,128)S(1)}, f32[2,3072]{1,0:T(2,128)}, u32[]{:S(2)}) copy-start(f32[2,3072]{1,0:T(2,128)} %param.7) | copy-start | bytes 73732
  2.9 8.3 %copy-start = (bf16[768,3072]{1,0:T(8,128)(2,1)S(1)}, bf16[768,3072]{1,0:T(8,128)(2,1)}, u32[]{:S(2)}) copy-start(bf16[768,3072]{1,0:T(8,128)(2,1)} %param.6) | copy-start | bytes 14155780
  2.9 57.4 %copy-start.8 = (f32[2,128]{1,0:T(2,128)S(1)}, f32[2,128]{1,0:T(2,128)}, u32[]{:S(2)}) copy-start(f32[2,128]{1,0:T(2,128)} %param.10) | copy-start | bytes 3076
  2.9 57.3 %collective-permute-start.1 = (bf16[768,3,512]{0,2,1:T(8,128)(2,1)S(1)}, bf16[768,3,512]{0,2,1:T(8,128)(2,1)}, u32[]{:S(2)}, u32[]{:S(2)}) collective-permute-start(bf16[768,3,512]{0,2,1:T(8,128)(2,1)S(1)} %copy.34), channel_id=1, source_target_pairs={{0,4},{4,8},{8,12},{12,0},{1,5},{5,9},{9,13},{13,1},{2,6},{6,10},{... | collective-permute-start | bytes 7077896 | tf_op jit(solution)/shard_map/ppermute | solution.py:16
  6.0 103.6 %collective-permute-start = (bf16[768,3,512]{0,2,1:T(8,128)(2,1)S(1)}, bf16[768,3,512]{0,2,1:T(8,128)(2,1)}, u32[]{:S(2)}, u32[]{:S(2)}) collective-permute-start(bf16[768,3,512]{0,2,1:T(8,128)(2,1)S(1)} %copy.34), channel_id=1, source_target_pairs={{0,12},{4,0},{8,4},{12,8},{1,13},{5,1},{9,5},{13,9},{2,14},{6,2},{... | collective-permute-start | bytes 7077896 | tf_op jit(solution)/shard_map/ppermute | solution.py:18
  60.2 100.3 %collective-permute-start.2 = (bf16[768,3,512]{0,2,1:T(8,128)(2,1)}, bf16[768,3,512]{0,2,1:T(8,128)(2,1)}, u32[]{:S(2)}, u32[]{:S(2)}) collective-permute-start(bf16[768,3,512]{0,2,1:T(8,128)(2,1)} %collective-permute-done.1), channel_id=1, source_target_pairs={{0,4},{4,8},{8,12},{12,0},{1,5},{5,9},{9,13},{13,1},{2,6},{6,10},{... | collective-permute-start | bytes 7077896 | tf_op jit(solution)/shard_map/ppermute | solution.py:16
  60.3 5.2 %copy-start.2 = (bf16[768,3,512]{2,0,1:T(8,128)(2,1)S(1)}, bf16[768,3,512]{2,0,1:T(8,128)(2,1)}, u32[]{:S(2)}) copy-start(bf16[768,3,512]{2,0,1:T(8,128)(2,1)} %param.8) | copy-start | bytes 7077892
  71.2 89.3 %copy-start.6 = (f32[3,512]{1,0:T(4,128)S(1)}, f32[3,512]{1,0:T(4,128)}, u32[]{:S(2)}) copy-start(f32[3,512]{1,0:T(4,128)} %param.9) | copy-start | bytes 18436
  168.5 13.5 %copy-start.9 = (s32[2,27]{1,0:T(2,128)S(1)}, s32[2,27]{1,0:T(2,128)}, u32[]{:S(2)}) copy-start(s32[2,27]{1,0:T(2,128)} %param.11) | copy-start | bytes 652
  174.9 36.0 %collective-permute-start.4 = (bf16[2,768,4,128]{3,1,2,0:T(8,128)(2,1)}, bf16[2,768,4,128]{3,1,2,0:T(8,128)(2,1)}, u32[]{:S(2)}, u32[]{:S(2)}) collective-permute-start(bf16[2,768,4,128]{3,1,2,0:T(8,128)(2,1)} %pad_maximum_fusion.1), channel_id=1, source_target_pairs={{4,0},{8,4},{12,8},{5,1},{9,5},{13,9},{6,2},{10,6},{14,10},{7,3},{... | collective-permute-start | bytes 4718600 | tf_op jit(solution)/shard_map/ppermute | solution.py:32
  176.2 35.9 %collective-permute-start.3 = (bf16[2,768,4,128]{3,1,2,0:T(8,128)(2,1)}, bf16[2,768,4,128]{3,1,2,0:T(8,128)(2,1)}, u32[]{:S(2)}, u32[]{:S(2)}) collective-permute-start(bf16[2,768,4,128]{3,1,2,0:T(8,128)(2,1)} %pad_maximum_fusion.1), channel_id=1, source_target_pairs={{0,4},{4,8},{8,12},{1,5},{5,9},{9,13},{2,6},{6,10},{10,14},{3,7},{... | collective-permute-start | bytes 4718600 | tf_op jit(solution)/shard_map/ppermute | solution.py:31
  191.1 23.0 %copy-start.3 = (pred[768,2304]{1,0:T(8,128)(4,1)S(1)}, pred[768,2304]{1,0:T(8,128)(4,1)}, u32[]{:S(2)}) copy-start(pred[768,2304]{1,0:T(8,128)(4,1)} %copy.38) | copy-start | bytes 5308420
  191.1 23.0 %copy-start.5 = (f32[768,4,128]{2,0,1:T(8,128)S(1)}, f32[768,4,128]{2,0,1:T(8,128)}, u32[]{:S(2)}) copy-start(f32[768,4,128]{2,0,1:T(8,128)} %copy.39) | copy-start | bytes 4718596
  214.1 12.9 %copy-start.1 = (bf16[2,2304,4,128]{3,1,2,0:T(8,128)(2,1)}, bf16[2,2304,4,128]{3,1,2,0:T(8,128)(2,1)S(1)}, u32[]{:S(2)}) copy-start(bf16[2,2304,4,128]{3,1,2,0:T(8,128)(2,1)S(1)} %pad_maximum_fusion) | copy-start | bytes 14155780
  214.1 12.9 %copy-start.4 = (pred[768,2304]{1,0:T(8,128)(4,1)S(1)}, pred[768,2304]{1,0:T(8,128)(4,1)}, u32[]{:S(2)}) copy-start(pred[768,2304]{1,0:T(8,128)(4,1)} %copy.38) | copy-start | bytes 5308420
